TPU v7x, 32 devices: a whole 2x2x4 slice. The times are simulated.
32 devices in a mesh: group: 2 (over y), frame: 4 (over z), row: 2 (over x), head: 2 (over core).
Axes of the slice: x: 2, y: 2, z: 4, core: 2. Of those that a mesh axis runs over, the one named last changes fastest.
Arguments:
- q_video: bfloat16 [16, 16, 16, 1536], P(('group', 'frame'), 'row', None, 'head'), parts along dimension 0, may hold values from -16 to 16
- k_video: bfloat16 [16, 16, 16, 1536], P(('group', 'frame'), 'row', None, 'head'), parts along dimension 0, may hold values from -8 to 8
- v_video: bfloat16 [16, 16, 16, 1536], P(('group', 'frame'), 'row', None, 'head'), parts along dimension 0, may hold values from -6 to 6
- q_reg: bfloat16 [256, 1536], P('group', 'head'), parts along dimension 0, may hold values from -16 to 16
- k_reg: bfloat16 [256, 1536], P('group', 'head'), parts along dimension 0, may hold values from -6 to 6
- v_reg: bfloat16 [256, 1536], P('group', 'head'), parts along dimension 0, may hold values from -6 to 6
- nbr_mask: int32 [4, 2, 2, 26], P('frame', 'row'), may hold values 0 or 1
Outputs:
- out_video: bfloat16 [16, 16, 16, 1536], P(('group', 'frame'), 'row', None, 'head'), parts along dimension 0
- out_reg: bfloat16 [256, 1536], P(('group', 'frame', 'row'), 'head'), parts along dimension 0
There are 2 independent parts, one for each index of `group`. A program takes and returns all parts, laid end to end along the dimension named above; an argument that names none is the same for every part. Nothing has to cross between parts.
All inputs are finite; a program needn't handle non-finite values. No bound on the sum of `nbr_mask` on one device may be relied on, other than what follows from the above.
Results may differ from a plain program's by a relative error of at most 0.0049.
Values may be sent and summed in bfloat16 or wider, within the bound.
A program may use at most 64 MiB of HBM per device.

v0:
```python
import jax
import jax.numpy as jnp
from jax import lax
from jax.sharding import PartitionSpec as P

HEAD_DIM = 128


def with_halo(array, sides, width):
    for axis, dim in sides:
        peers, length = (lax.axis_size(axis), array.shape[dim])
        up = [(i, (i + 1) % peers) for i in range(peers - 1)]
        down = [(j, i) for i, j in up]
        last = lax.slice_in_dim(array, length - width, length, axis=dim)
        first = lax.slice_in_dim(array, 0, width, axis=dim)
        before = lax.ppermute(last, axis, up)
        after = lax.ppermute(first, axis, down)
        array = jnp.concatenate([before, array, after], axis=dim)
    return array


def exact_product(weights, values):
    leading = weights.astype(values.dtype)
    remainder = (weights - leading.astype(weights.dtype)).astype(values.dtype)
    first = jnp.dot(leading, values, preferred_element_type=weights.dtype)
    return first + jnp.dot(remainder, values, preferred_element_type=weights.dtype)


def partial_softmax(query_rows, key_rows, value_rows, head_index, score_scale):
    query_head = lax.dynamic_slice_in_dim(query_rows, head_index * HEAD_DIM, HEAD_DIM, 1)
    key_head = lax.dynamic_slice_in_dim(key_rows, head_index * HEAD_DIM, HEAD_DIM, 1)
    value_head = lax.dynamic_slice_in_dim(value_rows, head_index * HEAD_DIM, HEAD_DIM, 1)
    scores = jnp.dot(query_head, key_head.T, preferred_element_type=jnp.float32) * score_scale
    row_max = jnp.max(scores, axis=-1)
    weights = jnp.exp(scores - row_max[:, None])
    weighted = exact_product(weights, value_head)
    return (row_max, jnp.sum(weights, axis=-1), weighted)


def per_head(query_rows, key_rows, value_rows, heads_dev, score_scale):

    def one_head(head_index):
        return partial_softmax(query_rows, key_rows, value_rows, head_index, score_scale)

    row_max, totals, weighted = lax.map(one_head, jnp.arange(heads_dev, dtype=jnp.int32))
    row_count = weighted.shape[1]
    return (
        row_max.T,
        totals.T,
        weighted.transpose(1, 0, 2).reshape(row_count, heads_dev * HEAD_DIM),
    )


def rescale(weighted, factor):
    row_count, heads_dev = factor.shape
    return (weighted.reshape(row_count, heads_dev, HEAD_DIM) * factor[:, :, None]).reshape(
        row_count, heads_dev * HEAD_DIM
    )


def combine(earlier, later):
    max_a, total_a, weighted_a = earlier
    max_b, total_b, weighted_b = later
    joint_max = jnp.maximum(max_a, max_b)
    factor_a = jnp.exp(max_a - joint_max)
    factor_b = jnp.exp(max_b - joint_max)
    return (
        joint_max,
        total_a * factor_a + total_b * factor_b,
        rescale(weighted_a, factor_a) + rescale(weighted_b, factor_b),
    )


def on_device(q_video, k_video, v_video, q_reg, k_reg, v_reg, nbr_mask):
    tile_f, tile_r, columns, features = q_video.shape
    col_tiles = nbr_mask.shape[2]
    tile_c = columns // col_tiles
    tile_size = tile_f * tile_r * tile_c
    heads_dev = features // HEAD_DIM
    registers = q_reg.shape[0]
    score_scale = HEAD_DIM ** (-0.5)
    frame_count = lax.axis_size("frame")
    rowdev_count = lax.axis_size("row")
    frame_pos = lax.axis_index("frame")
    rowdev_pos = lax.axis_index("row")
    paired = jnp.stack([k_video, v_video], 0)[None, None]
    near_block = with_halo(paired, (("frame", 0), ("row", 1)), 1)
    local_part = per_head(
        q_reg, k_video.reshape(-1, features), v_video.reshape(-1, features), heads_dev, score_scale
    )
    local_max, local_total, local_weighted = local_part
    row_share = registers // (frame_count * rowdev_count)
    row_start = (frame_pos * rowdev_count + rowdev_pos) * row_share
    own_queries = lax.dynamic_slice_in_dim(q_reg, row_start, row_share, 0)
    self_part = per_head(own_queries, k_reg, v_reg, heads_dev, score_scale)

    def own_rows(array):
        return lax.dynamic_slice_in_dim(array, row_start, row_share, 0)

    global_max = lax.pmax(local_max, ("frame", "row"))
    factor = jnp.exp(local_max - global_max)
    reduced = lax.psum((rescale(local_weighted, factor), local_total * factor), ("frame", "row"))
    collected = (own_rows(global_max), own_rows(reduced[1]), own_rows(reduced[0]))
    final_max, final_total, final_weighted = combine(collected, self_part)
    out_reg = (
        (final_weighted.reshape(row_share, heads_dev, HEAD_DIM) / final_total[:, :, None])
        .reshape(row_share, features)
        .astype(jnp.bfloat16)
    )
    near_block = near_block.reshape(3, 3, 2, tile_f, tile_r, col_tiles, tile_c, features)
    queries = (
        q_video.reshape(tile_f, tile_r, col_tiles, tile_c, features)
        .transpose(2, 0, 1, 3, 4)
        .reshape(col_tiles, tile_size, features)
    )
    window = min(3, col_tiles)
    full_mask = jnp.concatenate(
        [nbr_mask[0, 0, :, :13], jnp.ones((col_tiles, 1), jnp.int32), nbr_mask[0, 0, :, 13:]], 1
    )
    offsets = jnp.arange(3, dtype=jnp.int32) - 1
    frame_inside = (frame_pos + offsets >= 0) & (frame_pos + offsets < frame_count)
    row_inside = (rowdev_pos + offsets >= 0) & (rowdev_pos + offsets < rowdev_count)

    def one_item(item_index):
        col_index = item_index // heads_dev
        head_index = item_index % heads_dev
        first_col = jnp.clip(col_index - 1, 0, col_tiles - window)
        anchor = jnp.zeros((), jnp.int32)
        near_piece = lax.dynamic_slice(
            near_block,
            (anchor, anchor, anchor, anchor, anchor, first_col, anchor, head_index * HEAD_DIM),
            (3, 3, 2, tile_f, tile_r, window, tile_c, HEAD_DIM),
        )
        near_head = near_piece.transpose(2, 0, 1, 5, 3, 4, 6, 7).reshape(
            2, 3, 3, window, tile_size, HEAD_DIM
        )
        key_cols = first_col + jnp.arange(window, dtype=jnp.int32)
        offset_codes = (
            (offsets[:, None, None] + 1) * 9
            + (offsets[None, :, None] + 1) * 3
            + (key_cols - col_index + 1)[None, None, :]
        )
        mask_row = lax.dynamic_index_in_dim(full_mask, col_index, 0, keepdims=False)
        picked = jnp.sum(
            jnp.where(offset_codes[..., None] == jnp.arange(27, dtype=jnp.int32), mask_row, 0),
            axis=-1,
        )
        adjacent = jnp.abs(key_cols - col_index) <= 1
        allowed = (
            (picked == 1)
            & frame_inside[:, None, None]
            & row_inside[None, :, None]
            & adjacent[None, None, :]
        )
        key_ok = jnp.concatenate(
            [
                jnp.repeat(
                    allowed.reshape(-1), tile_size, total_repeat_length=9 * window * tile_size
                ),
                jnp.ones((registers,), bool),
            ]
        )
        key_rows = jnp.concatenate(
            [
                near_head[0].reshape(-1, HEAD_DIM),
                lax.dynamic_slice_in_dim(k_reg, head_index * HEAD_DIM, HEAD_DIM, 1),
            ],
            0,
        )
        value_rows = jnp.concatenate(
            [
                near_head[1].reshape(-1, HEAD_DIM),
                lax.dynamic_slice_in_dim(v_reg, head_index * HEAD_DIM, HEAD_DIM, 1),
            ],
            0,
        )
        query_head = lax.dynamic_slice(
            queries, (col_index, anchor, head_index * HEAD_DIM), (1, tile_size, HEAD_DIM)
        )[0]
        scores = jnp.dot(query_head, key_rows.T, preferred_element_type=jnp.float32) * score_scale
        scores = jnp.where(key_ok[None, :], scores, -jnp.inf)
        weights = jax.nn.softmax(scores, axis=-1).astype(jnp.bfloat16)
        return jnp.dot(weights, value_rows, preferred_element_type=jnp.float32).astype(jnp.bfloat16)

    results = lax.map(one_item, jnp.arange(col_tiles * heads_dev, dtype=jnp.int32))
    out_video = (
        results.reshape(col_tiles, heads_dev, tile_f, tile_r, tile_c, HEAD_DIM)
        .transpose(2, 3, 0, 4, 1, 5)
        .reshape(tile_f, tile_r, columns, features)
    )
    return (out_video, out_reg)


def solution(mesh):
    return jax.shard_map(
        on_device,
        mesh=mesh,
        in_specs=(
            P(("group", "frame"), "row", None, "head"),
            P(("group", "frame"), "row", None, "head"),
            P(("group", "frame"), "row", None, "head"),
            P("group", "head"),
            P("group", "head"),
            P("group", "head"),
            P("frame", "row", None, None),
        ),
        out_specs=(
            P(("group", "frame"), "row", None, "head"),
            P(("group", "frame", "row"), "head"),
        ),
        check_vma=False,
    )
```

profile of v0, /device:TPU:0, one launch (start us, length us, event | category | flops | bytes accessed | tf_op | source)
XLA Modules:
  0.0 386.3 jit_solution(3703701731983514804)
XLA Ops:
  8.4 5.0 %collective-permute-start = (bf16[1,1,2,2,8,16,768]{6,5,4,3,2,1,0:T(8,128)(2,1)S(1)}, bf16[1,1,2,2,8,16,768]{6,5,4,3,2,1,0:T(8,128)(2,1)S(1)}, u32[]{:S(2)}, u32[]{:S(2)}) collective-permute-start(bf16[1,1,2,2,8,16,768]{6,5,4,3,2,1,0:T(8,128)(2,1)S(1)} %maximum_bitcast_fusion.1), channel_id=1, source_target_pairs={{0,4},{4,8},{8,12},{1,5},{5,9},{9,13},{2,6},{6,10},{10,14},{3,7},{... | collective-permute-start | bytes 2359304 | tf_op jit(solution)/shard_map/ppermute | solution.py:16
  14.7 29.3 %while.46 = (s32[]{:T(128)}, f32[6,128]{1,0:T(8,128)S(1)}, f32[6,128]{1,0:T(8,128)S(1)}, f32[6,128,128]{1,2,0:T(8,128)S(1)}, s32[6]{0:T(128)S(1)}, /*index=5*/bf...) while((s32[]{:T(128)}, f32[6,128]{1,0:T(8,128)S(1)}, ...), condition=%wide.region_8.9_spmd, body=%wide.region_5.0_spmd.sunk | while | flops 25542404 | bytes 1218243 | solution.py:45
  44.0 22.7 %pmax.7 = f32[128,6]{0,1:T(8,128)S(1)} all-reduce(f32[128,6]{0,1:T(8,128)S(1)} %bitcast.239), channel_id=1, replica_groups=mesh['group'=2,'frame'=4,'row'=2,'head'=2] {'frame','row'}, use_global_device_ids=true, to_apply=%region_9.10 | all-reduce | flops 768 | bytes 6144 | tf_op jit(solution)/shard_map/pmax | solution.py:100
  74.4 17.6 %while.47 = (s32[]{:T(128)}, f32[6,16]{1,0:T(8,128)S(1)}, f32[6,16]{1,0:T(8,128)S(1)}, f32[6,16,128]{2,1,0:T(8,128)S(1)}, s32[6]{0:T(128)S(1)}, /*index=5*/bf16[...) while((s32[]{:T(128)}, f32[6,16]{1,0:T(8,128)S(1)}, ...), condition=%wide.region_14.15_spmd, body=%wide.region_11.14_spmd.sunk | while | flops 1597414 | bytes 162435 | solution.py:45
  92.0 43.7 %psum.15 = f32[128,6]{0,1:T(8,128)S(1)} all-reduce(f32[128,6]{0,1:T(8,128)S(1)} %get-tuple-element.582), channel_id=1, replica_groups=mesh['group'=2,'frame'=4,'row'=2,'head'=2] {'frame','row'}, use_global_device_ids=true, to_apply=%region_15.16 | all-reduce | flops 768 | bytes 6144 | tf_op jit(solution)/shard_map/psum | solution.py:102
  139.1 5.9 %maximum_bitcast_fusion = bf16[3,3,2,2,8,2,8,768]{7,6,5,4,3,2,1,0:T(8,128)(2,1)} fusion(bf16[3,1,2,2,8,16,768]{6,5,4,3,2,1,0:T(8,128)(2,1)} %collective-permute-done.3, bf16[1,1,2,2,8,16,768]{6,5,4,3,2,1,0:T(8,128)(2,1)S(1)} %collective-permute-done.1, bf16[1,1,2,2,8,16,768]{6,5,4,3,2,1,0:T(8,128)(2,1)S(1)} %maximum_bitcast_fusion.1, ...), kind=kLoop, calls=%fused_computation.100 | loop fusion | flops 14155776 | bytes 14155776 | tf_op jit(solution)/shard_map/reshape | solution.py:110
  145.0 233.7 %while.48 = (s32[]{:T(128)}, bf16[12,128,128]{2,1,0:T(8,128)(2,1)S(1)}, s32[12]{0:T(128)S(1)}, s32[2,27]{1,0:T(2,128)S(1)}, bf16[2,128,768]{2,1,0:T(8,128)(2,1)S...) while((s32[]{:T(128)}, ...), condition=%wide.region_4.5_spmd.clone, body=%wide.region_0.4_spmd.clone.sunk | while | flops 164492608 | bytes 10002113 | solution.py:185
  149.0 4.7 %select_reduce_fusion.2 = (pred[2304]{0:T(1024)(128)(4,1)S(1)}, pred[2304]{0:T(1024)(128)(4,1)S(1)}, pred[2304]{0:T(1024)(128)(4,1)S(1)}, pred[2304]{0:T(1024)(1...) fusion(pred[]{:T(512)} %bitcast.204, ...), kind=kLoop, calls=%fused_computation.55.clone.1 | loop fusion | flops 57600 | bytes 46087 | tf_op jit(solution)/shard_map/while/body/eval_jaxpr/jit(_take)/gather | solution.py:157
  153.7 7.0 %fusion.121 = pred[2304]{0:T(1024)(128)(4,1)S(1)} fusion(pred[2304]{0:T(1024)(128)(4,1)S(1)} %get-tuple-element.846, pred[2304]{0:T(1024)(128)(4,1)S(1)} %get-tuple-element.847, pred[2304]{0:T(1024)(128)(4,1)S(1)} %get-tuple-element.848, pred[2304]{0:T(1024)(128)(4,1)S(1)} %get-tuple-element.849, pred[2304]{0:T(1024)(128)(4,1)S(1)} %get-tuple-element.850, ...), kind=kLoop, calls=%fused_computation.79.clone.1 | loop fusion | flops 46080 | bytes 29963 | tf_op jit(solution)/shard_map/while/body/eval_jaxpr/jit(_take)/select_n | solution.py:157
  168.5 4.7 %select_reduce_fusion.2 = (pred[2304]{0:T(1024)(128)(4,1)S(1)}, pred[2304]{0:T(1024)(128)(4,1)S(1)}, pred[2304]{0:T(1024)(128)(4,1)S(1)}, pred[2304]{0:T(1024)(1...) fusion(pred[]{:T(512)} %bitcast.204, ...), kind=kLoop, calls=%fused_computation.55.clone.1 | loop fusion | flops 57600 | bytes 46087 | tf_op jit(solution)/shard_map/while/body/eval_jaxpr/jit(_take)/gather | solution.py:157
  173.2 7.0 %fusion.121 = pred[2304]{0:T(1024)(128)(4,1)S(1)} fusion(pred[2304]{0:T(1024)(128)(4,1)S(1)} %get-tuple-element.846, pred[2304]{0:T(1024)(128)(4,1)S(1)} %get-tuple-element.847, pred[2304]{0:T(1024)(128)(4,1)S(1)} %get-tuple-element.848, pred[2304]{0:T(1024)(128)(4,1)S(1)} %get-tuple-element.849, pred[2304]{0:T(1024)(128)(4,1)S(1)} %get-tuple-element.850, ...), kind=kLoop, calls=%fused_computation.79.clone.1 | loop fusion | flops 46080 | bytes 29963 | tf_op jit(solution)/shard_map/while/body/eval_jaxpr/jit(_take)/select_n | solution.py:157
  187.9 4.7 %select_reduce_fusion.2 = (pred[2304]{0:T(1024)(128)(4,1)S(1)}, pred[2304]{0:T(1024)(128)(4,1)S(1)}, pred[2304]{0:T(1024)(128)(4,1)S(1)}, pred[2304]{0:T(1024)(1...) fusion(pred[]{:T(512)} %bitcast.204, ...), kind=kLoop, calls=%fused_computation.55.clone.1 | loop fusion | flops 57600 | bytes 46087 | tf_op jit(solution)/shard_map/while/body/eval_jaxpr/jit(_take)/gather | solution.py:157
  192.6 7.0 %fusion.121 = pred[2304]{0:T(1024)(128)(4,1)S(1)} fusion(pred[2304]{0:T(1024)(128)(4,1)S(1)} %get-tuple-element.846, pred[2304]{0:T(1024)(128)(4,1)S(1)} %get-tuple-element.847, pred[2304]{0:T(1024)(128)(4,1)S(1)} %get-tuple-element.848, pred[2304]{0:T(1024)(128)(4,1)S(1)} %get-tuple-element.849, pred[2304]{0:T(1024)(128)(4,1)S(1)} %get-tuple-element.850, ...), kind=kLoop, calls=%fused_computation.79.clone.1 | loop fusion | flops 46080 | bytes 29963 | tf_op jit(solution)/shard_map/while/body/eval_jaxpr/jit(_take)/select_n | solution.py:157
  207.4 4.7 %select_reduce_fusion.2 = (pred[2304]{0:T(1024)(128)(4,1)S(1)}, pred[2304]{0:T(1024)(128)(4,1)S(1)}, pred[2304]{0:T(1024)(128)(4,1)S(1)}, pred[2304]{0:T(1024)(1...) fusion(pred[]{:T(512)} %bitcast.204, ...), kind=kLoop, calls=%fused_computation.55.clone.1 | loop fusion | flops 57600 | bytes 46087 | tf_op jit(solution)/shard_map/while/body/eval_jaxpr/jit(_take)/gather | solution.py:157
  212.1 7.0 %fusion.121 = pred[2304]{0:T(1024)(128)(4,1)S(1)} fusion(pred[2304]{0:T(1024)(128)(4,1)S(1)} %get-tuple-element.846, pred[2304]{0:T(1024)(128)(4,1)S(1)} %get-tuple-element.847, pred[2304]{0:T(1024)(128)(4,1)S(1)} %get-tuple-element.848, pred[2304]{0:T(1024)(128)(4,1)S(1)} %get-tuple-element.849, pred[2304]{0:T(1024)(128)(4,1)S(1)} %get-tuple-element.850, ...), kind=kLoop, calls=%fused_computation.79.clone.1 | loop fusion | flops 46080 | bytes 29963 | tf_op jit(solution)/shard_map/while/body/eval_jaxpr/jit(_take)/select_n | solution.py:157
  231.6 7.0 %fusion.121 = pred[2304]{0:T(1024)(128)(4,1)S(1)} fusion(pred[2304]{0:T(1024)(128)(4,1)S(1)} %get-tuple-element.846, pred[2304]{0:T(1024)(128)(4,1)S(1)} %get-tuple-element.847, pred[2304]{0:T(1024)(128)(4,1)S(1)} %get-tuple-element.848, pred[2304]{0:T(1024)(128)(4,1)S(1)} %get-tuple-element.849, pred[2304]{0:T(1024)(128)(4,1)S(1)} %get-tuple-element.850, ...), kind=kLoop, calls=%fused_computation.79.clone.1 | loop fusion | flops 46080 | bytes 29963 | tf_op jit(solution)/shard_map/while/body/eval_jaxpr/jit(_take)/select_n | solution.py:157
  251.1 7.0 %fusion.121 = pred[2304]{0:T(1024)(128)(4,1)S(1)} fusion(pred[2304]{0:T(1024)(128)(4,1)S(1)} %get-tuple-element.846, pred[2304]{0:T(1024)(128)(4,1)S(1)} %get-tuple-element.847, pred[2304]{0:T(1024)(128)(4,1)S(1)} %get-tuple-element.848, pred[2304]{0:T(1024)(128)(4,1)S(1)} %get-tuple-element.849, pred[2304]{0:T(1024)(128)(4,1)S(1)} %get-tuple-element.850, ...), kind=kLoop, calls=%fused_computation.79.clone.1 | loop fusion | flops 46080 | bytes 29963 | tf_op jit(solution)/shard_map/while/body/eval_jaxpr/jit(_take)/select_n | solution.py:157
  265.8 4.7 %select_reduce_fusion.2 = (pred[2304]{0:T(1024)(128)(4,1)S(1)}, pred[2304]{0:T(1024)(128)(4,1)S(1)}, pred[2304]{0:T(1024)(128)(4,1)S(1)}, pred[2304]{0:T(1024)(1...) fusion(pred[]{:T(512)} %bitcast.204, ...), kind=kLoop, calls=%fused_computation.55.clone.1 | loop fusion | flops 57600 | bytes 46087 | tf_op jit(solution)/shard_map/while/body/eval_jaxpr/jit(_take)/gather | solution.py:157
  270.5 7.0 %fusion.121 = pred[2304]{0:T(1024)(128)(4,1)S(1)} fusion(pred[2304]{0:T(1024)(128)(4,1)S(1)} %get-tuple-element.846, pred[2304]{0:T(1024)(128)(4,1)S(1)} %get-tuple-element.847, pred[2304]{0:T(1024)(128)(4,1)S(1)} %get-tuple-element.848, pred[2304]{0:T(1024)(128)(4,1)S(1)} %get-tuple-element.849, pred[2304]{0:T(1024)(128)(4,1)S(1)} %get-tuple-element.850, ...), kind=kLoop, calls=%fused_computation.79.clone.1 | loop fusion | flops 46080 | bytes 29963 | tf_op jit(solution)/shard_map/while/body/eval_jaxpr/jit(_take)/select_n | solution.py:157
  290.0 7.0 %fusion.121 = pred[2304]{0:T(1024)(128)(4,1)S(1)} fusion(pred[2304]{0:T(1024)(128)(4,1)S(1)} %get-tuple-element.846, pred[2304]{0:T(1024)(128)(4,1)S(1)} %get-tuple-element.847, pred[2304]{0:T(1024)(128)(4,1)S(1)} %get-tuple-element.848, pred[2304]{0:T(1024)(128)(4,1)S(1)} %get-tuple-element.849, pred[2304]{0:T(1024)(128)(4,1)S(1)} %get-tuple-element.850, ...), kind=kLoop, calls=%fused_computation.79.clone.1 | loop fusion | flops 46080 | bytes 29963 | tf_op jit(solution)/shard_map/while/body/eval_jaxpr/jit(_take)/select_n | solution.py:157
  309.5 7.0 %fusion.121 = pred[2304]{0:T(1024)(128)(4,1)S(1)} fusion(pred[2304]{0:T(1024)(128)(4,1)S(1)} %get-tuple-element.846, pred[2304]{0:T(1024)(128)(4,1)S(1)} %get-tuple-element.847, pred[2304]{0:T(1024)(128)(4,1)S(1)} %get-tuple-element.848, pred[2304]{0:T(1024)(128)(4,1)S(1)} %get-tuple-element.849, pred[2304]{0:T(1024)(128)(4,1)S(1)} %get-tuple-element.850, ...), kind=kLoop, calls=%fused_computation.79.clone.1 | loop fusion | flops 46080 | bytes 29963 | tf_op jit(solution)/shard_map/while/body/eval_jaxpr/jit(_take)/select_n | solution.py:157
  329.0 7.0 %fusion.121 = pred[2304]{0:T(1024)(128)(4,1)S(1)} fusion(pred[2304]{0:T(1024)(128)(4,1)S(1)} %get-tuple-element.846, pred[2304]{0:T(1024)(128)(4,1)S(1)} %get-tuple-element.847, pred[2304]{0:T(1024)(128)(4,1)S(1)} %get-tuple-element.848, pred[2304]{0:T(1024)(128)(4,1)S(1)} %get-tuple-element.849, pred[2304]{0:T(1024)(128)(4,1)S(1)} %get-tuple-element.850, ...), kind=kLoop, calls=%fused_computation.79.clone.1 | loop fusion | flops 46080 | bytes 29963 | tf_op jit(solution)/shard_map/while/body/eval_jaxpr/jit(_take)/select_n | solution.py:157
  348.4 7.0 %fusion.121 = pred[2304]{0:T(1024)(128)(4,1)S(1)} fusion(pred[2304]{0:T(1024)(128)(4,1)S(1)} %get-tuple-element.846, pred[2304]{0:T(1024)(128)(4,1)S(1)} %get-tuple-element.847, pred[2304]{0:T(1024)(128)(4,1)S(1)} %get-tuple-element.848, pred[2304]{0:T(1024)(128)(4,1)S(1)} %get-tuple-element.849, pred[2304]{0:T(1024)(128)(4,1)S(1)} %get-tuple-element.850, ...), kind=kLoop, calls=%fused_computation.79.clone.1 | loop fusion | flops 46080 | bytes 29963 | tf_op jit(solution)/shard_map/while/body/eval_jaxpr/jit(_take)/select_n | solution.py:157
  367.9 7.0 %fusion.121 = pred[2304]{0:T(1024)(128)(4,1)S(1)} fusion(pred[2304]{0:T(1024)(128)(4,1)S(1)} %get-tuple-element.846, pred[2304]{0:T(1024)(128)(4,1)S(1)} %get-tuple-element.847, pred[2304]{0:T(1024)(128)(4,1)S(1)} %get-tuple-element.848, pred[2304]{0:T(1024)(128)(4,1)S(1)} %get-tuple-element.849, pred[2304]{0:T(1024)(128)(4,1)S(1)} %get-tuple-element.850, ...), kind=kLoop, calls=%fused_computation.79.clone.1 | loop fusion | flops 46080 | bytes 29963 | tf_op jit(solution)/shard_map/while/body/eval_jaxpr/jit(_take)/select_n | solution.py:157
  (388 shorter events, 153.9 us)
Async XLA Ops:
  7.2 130.2 %all-reduce.3.cloned.1.call-start = ((), (), s32[]{:S(2)}) async-start(), calls=%async_computation | async-start | bytes 786432 | tf_op jit(solution)/shard_map/psum | solution.py:102
  8.4 60.2 %collective-permute-start = (bf16[1,1,2,2,8,16,768]{6,5,4,3,2,1,0:T(8,128)(2,1)S(1)}, bf16[1,1,2,2,8,16,768]{6,5,4,3,2,1,0:T(8,128)(2,1)S(1)}, u32[]{:S(2)}, u32[]{:S(2)}) collective-permute-start(bf16[1,1,2,2,8,16,768]{6,5,4,3,2,1,0:T(8,128)(2,1)S(1)} %maximum_bitcast_fusion.1), channel_id=1, source_target_pairs={{0,4},{4,8},{8,12},{1,5},{5,9},{9,13},{2,6},{6,10},{10,14},{3,7},{... | collective-permute-start | bytes 2359304 | tf_op jit(solution)/shard_map/ppermute | solution.py:16
  13.4 55.2 %collective-permute-start.1 = (bf16[1,1,2,2,8,16,768]{6,5,4,3,2,1,0:T(8,128)(2,1)S(1)}, bf16[1,1,2,2,8,16,768]{6,5,4,3,2,1,0:T(8,128)(2,1)S(1)}, u32[]{:S(2)}, u32[]{:S(2)}) collective-permute-start(bf16[1,1,2,2,8,16,768]{6,5,4,3,2,1,0:T(8,128)(2,1)S(1)} %maximum_bitcast_fusion.1), channel_id=1, source_target_pairs={{4,0},{8,4},{12,8},{5,1},{9,5},{13,9},{6,2},{10,6},{14,10},{7,3},{... | collective-permute-start | bytes 2359304 | tf_op jit(solution)/shard_map/ppermute | solution.py:17
  68.5 5.8 %copy-start.2 = (bf16[128,768]{1,0:T(8,128)(2,1)S(1)}, bf16[128,768]{1,0:T(8,128)(2,1)}, u32[]{:S(2)}) copy-start(bf16[128,768]{1,0:T(8,128)(2,1)} %param.20) | copy-start | bytes 589828
  68.6 67.5 %copy-start = (bf16[2,8,16,768]{3,2,1,0:T(8,128)(2,1)S(1)}, bf16[2,8,16,768]{3,2,1,0:T(8,128)(2,1)}, u32[]{:S(2)}) copy-start(bf16[2,8,16,768]{3,2,1,0:T(8,128)(2,1)} %param.15) | copy-start | bytes 1179652
  70.2 65.8 %copy-start.3 = (s32[1,1,2,26]{3,2,1,0:T(2,128)S(1)}, s32[1,1,2,26]{3,2,1,0:T(2,128)}, u32[]{:S(2)}) copy-start(s32[1,1,2,26]{3,2,1,0:T(2,128)} %param.21) | copy-start | bytes 628
  70.2 68.8 %collective-permute-start.2 = (bf16[3,1,2,2,8,16,768]{6,5,4,3,2,1,0:T(8,128)(2,1)}, bf16[3,1,2,2,8,16,768]{6,5,4,3,2,1,0:T(8,128)(2,1)}, u32[]{:S(2)}, u32[]{:S(2)}) collective-permute-start(bf16[3,1,2,2,8,16,768]{6,5,4,3,2,1,0:T(8,128)(2,1)} %pad_maximum_fusion), channel_id=1, source_target_pairs={{0,2},{1,3},{4,6},{5,7},{8,10},{9,11},{12,14},{13,15},{16,18},{17,... | collective-permute-start | bytes 7077896 | tf_op jit(solution)/shard_map/ppermute | solution.py:16
  73.1 66.0 %collective-permute-start.3 = (bf16[3,1,2,2,8,16,768]{6,5,4,3,2,1,0:T(8,128)(2,1)}, bf16[3,1,2,2,8,16,768]{6,5,4,3,2,1,0:T(8,128)(2,1)}, u32[]{:S(2)}, u32[]{:S(2)}) collective-permute-start(bf16[3,1,2,2,8,16,768]{6,5,4,3,2,1,0:T(8,128)(2,1)} %pad_maximum_fusion), channel_id=1, source_target_pairs={{2,0},{3,1},{6,4},{7,5},{10,8},{11,9},{14,12},{15,13},{18,16},{19,... | collective-permute-start | bytes 7077896 | tf_op jit(solution)/shard_map/ppermute | solution.py:17
  139.1 5.9 %copy-start.1 = (bf16[12,128,128]{2,1,0:T(8,128)(2,1)S(1)}, bf16[12,128,128]{2,1,0:T(8,128)(2,1)}, u32[]{:S(2)}) copy-start(bf16[12,128,128]{2,1,0:T(8,128)(2,1)} %custom-call.6) | copy-start | bytes 1179652
Sparse Core Ops, SparseCore 0:
  67.9 69.4 all-reduce.2
where the time goes:
time: 392 us; the launch traced here: 386 us
  other arithmetic  164 us (42%)
  blocking collectives  66.4 us (17%)
  local copies, waits for them, and re-layouts  58.4 us (15%)
  matrix products  38.3 us (10%)
  loops' own time  33.3 us (8%)
  between operations  14.2 us (4%)
  starting transfers between devices  10.4 us (3%)
    select_n x12, other arithmetic, one_item(): jnp.repeat(allowed.reshape(-1), tile_size, total_repeat_length=9 * window...  84.1 us
    gather x12, other arithmetic, one_item(): jnp.repeat(allowed.reshape(-1), tile_size, total_repeat_length=9 * window...  56.4 us
    psum x1, blocking collectives, on_device(): lax.psum((rescale(local_weighted, factor), local_total * factor), ('frame...  43.7 us
    another operation x1, loops' own time, on_device(): lax.map(one_item, jnp.arange(col_tiles * heads_dev, dtype=jnp.int32))  25 us
    pmax x1, blocking collectives, on_device(): global_max = lax.pmax(local_max, ('frame', 'row'))  22.7 us
    transpose x12, local copies, waits for them, and re-layouts, one_item(): near_piece.transpose(2, 0, 1, 5, 3, 4, 6, 7)  18.9 us
    dot_general x12, matrix products, partial_softmax(): jnp.dot(query_head, key_head.T, preferred_element_type=jnp.float32)  12.8 us
    dynamic_slice x12, local copies, waits for them, and re-layouts, one_item(): lax.dynamic_slice_in_dim(v_reg, head_index * HEAD_DIM, HEAD_DIM, 1)  9.27 us
  transfers between devices with their start and end apart: 5, of which 1 were waited for; matrix products, arithmetic and copies ran while one was open for 11% of the time, Pallas kernels for 0%

commit v1 on v0

--- a/solution.py
+++ b/solution.py
@@ -99,7 +99,8 @@
 
     global_max = lax.pmax(local_max, ("frame", "row"))
     factor = jnp.exp(local_max - global_max)
-    reduced = lax.psum((rescale(local_weighted, factor), local_total * factor), ("frame", "row"))
+    half = lax.psum((rescale(local_weighted, factor), local_total * factor), "row")
+    reduced = lax.psum(half, "frame")
     collected = (own_rows(global_max), own_rows(reduced[1]), own_rows(reduced[0]))
     final_max, final_total, final_weighted = combine(collected, self_part)
     out_reg = (

time: 392 us -> 431 us (1.099)
  waiting for transfers between devices: 1.19 us -> 34.4 us
  blocking collectives: 66.4 us -> 72.4 us
    psum x1 -> x2, waiting for transfers between devices: 1.16 us -> 34.3 us  [the longest x1 34.3 us: on_device(): reduced = lax.psum(half, 'frame')]
    psum x1 -> x2, blocking collectives: 43.7 us -> 49.7 us  [the longest x1 39.7 us: on_device(): lax.psum((rescale(local_weighted, factor), local_total * factor), 'row')]
  transfers between devices with their start and end apart: 5 -> 6, of which waited for: 1 -> 1; matrix products, arithmetic and copies ran while one was open for 11% -> 10% of each run, Pallas kernels for 0% -> 0%
where the time goes in v1:
time: 431 us; the launch traced here: 425 us
  other arithmetic  164 us (38%)
  blocking collectives  72.4 us (17%)
  local copies, waits for them, and re-layouts  58.1 us (13%)
  matrix products  38.3 us (9%)
  waiting for transfers between devices  34.4 us (8%)
  loops' own time  33.3 us (8%)
  between operations  14.2 us (3%)
  starting transfers between devices  10.4 us (2%)
    select_n x12, other arithmetic, one_item(): jnp.repeat(allowed.reshape(-1), tile_size, total_repeat_length=9 * window...  84.1 us
    gather x12, other arithmetic, one_item(): jnp.repeat(allowed.reshape(-1), tile_size, total_repeat_length=9 * window...  56.4 us
    psum x1, blocking collectives, on_device(): lax.psum((rescale(local_weighted, factor), local_total * factor), 'row')  39.7 us
    psum x1, waiting for transfers between devices, on_device(): reduced = lax.psum(half, 'frame')  34.3 us
    another operation x1, loops' own time, on_device(): lax.map(one_item, jnp.arange(col_tiles * heads_dev, dtype=jnp.int32))  25 us
    pmax x1, blocking collectives, on_device(): global_max = lax.pmax(local_max, ('frame', 'row'))  22.7 us
    transpose x12, local copies, waits for them, and re-layouts, one_item(): near_piece.transpose(2, 0, 1, 5, 3, 4, 6, 7)  18.9 us
    dot_general x12, matrix products, partial_softmax(): jnp.dot(query_head, key_head.T, preferred_element_type=jnp.float32)  12.8 us
  transfers between devices with their start and end apart: 6, of which 1 were waited for; matrix products, arithmetic and copies ran while one was open for 10% of the time, Pallas kernels for 0%

profile of v1, /device:TPU:0, one launch (start us, length us, event | category | flops | bytes accessed | tf_op | source)
XLA Modules:
  0.0 425.3 jit_solution(8674074670416610129)
XLA Ops:
  8.4 5.0 %collective-permute-start = (bf16[1,1,2,2,8,16,768]{6,5,4,3,2,1,0:T(8,128)(2,1)S(1)}, bf16[1,1,2,2,8,16,768]{6,5,4,3,2,1,0:T(8,128)(2,1)S(1)}, u32[]{:S(2)}, u32[]{:S(2)}) collective-permute-start(bf16[1,1,2,2,8,16,768]{6,5,4,3,2,1,0:T(8,128)(2,1)S(1)} %maximum_bitcast_fusion.1), channel_id=1, source_target_pairs={{0,4},{4,8},{8,12},{1,5},{5,9},{9,13},{2,6},{6,10},{10,14},{3,7},{... | collective-permute-start | bytes 2359304 | tf_op jit(solution)/shard_map/ppermute | solution.py:16
  14.7 29.3 %while.46 = (s32[]{:T(128)}, f32[6,128]{1,0:T(8,128)S(1)}, f32[6,128]{1,0:T(8,128)S(1)}, f32[6,128,128]{1,2,0:T(8,128)S(1)}, s32[6]{0:T(128)S(1)}, /*index=5*/bf...) while((s32[]{:T(128)}, f32[6,128]{1,0:T(8,128)S(1)}, ...), condition=%wide.region_8.9_spmd, body=%wide.region_5.0_spmd.sunk | while | flops 25542404 | bytes 1218243 | solution.py:45
  44.0 22.7 %pmax.7 = f32[128,6]{0,1:T(8,128)S(1)} all-reduce(f32[128,6]{0,1:T(8,128)S(1)} %bitcast.239), channel_id=1, replica_groups=mesh['group'=2,'frame'=4,'row'=2,'head'=2] {'frame','row'}, use_global_device_ids=true, to_apply=%region_9.10 | all-reduce | flops 768 | bytes 6144 | tf_op jit(solution)/shard_map/pmax | solution.py:100
  74.4 17.6 %while.47 = (s32[]{:T(128)}, f32[6,16]{1,0:T(8,128)S(1)}, f32[6,16]{1,0:T(8,128)S(1)}, f32[6,16,128]{2,1,0:T(8,128)S(1)}, s32[6]{0:T(128)S(1)}, /*index=5*/bf16[...) while((s32[]{:T(128)}, f32[6,16]{1,0:T(8,128)S(1)}, ...), condition=%wide.region_15.16_spmd, body=%wide.region_12.15_spmd.sunk | while | flops 1597414 | bytes 162435 | solution.py:45
  92.0 39.7 %psum.30 = f32[128,6]{0,1:T(8,128)S(1)} all-reduce(f32[128,6]{0,1:T(8,128)S(1)} %get-tuple-element.582), channel_id=1, replica_groups=mesh['group'=2,'frame'=4,'row'=2,'head'=2] {'row'}, use_global_device_ids=true, to_apply=%region_16.17 | all-reduce | flops 768 | bytes 6144 | tf_op jit(solution)/shard_map/psum | solution.py:102
  131.7 10.1 %psum.31 = f32[128,6]{0,1:T(8,128)S(1)} all-reduce(f32[128,6]{0,1:T(8,128)S(1)} %psum.30), channel_id=1, replica_groups=mesh['group'=2,'frame'=4,'row'=2,'head'=2] {'frame'}, use_global_device_ids=true, to_apply=%region_17.18 | all-reduce | flops 768 | bytes 6144 | tf_op jit(solution)/shard_map/psum | solution.py:103
  142.3 34.3 %all-reduce.6.cloned.1.call-done = f32[128,768]{1,0:T(8,128)} async-done(((f32[128,768]{1,0:T(8,128)}), f32[128,768]{1,0:T(8,128)}) %all-reduce.6.cloned.1.call-update) | async-done | bytes 393232 | tf_op jit(solution)/shard_map/psum | solution.py:103
  178.3 5.9 %maximum_bitcast_fusion = bf16[3,3,2,2,8,2,8,768]{7,6,5,4,3,2,1,0:T(8,128)(2,1)} fusion(bf16[3,1,2,2,8,16,768]{6,5,4,3,2,1,0:T(8,128)(2,1)} %collective-permute-done.3, bf16[1,1,2,2,8,16,768]{6,5,4,3,2,1,0:T(8,128)(2,1)S(1)} %collective-permute-done.1, bf16[1,1,2,2,8,16,768]{6,5,4,3,2,1,0:T(8,128)(2,1)S(1)} %maximum_bitcast_fusion.1, ...), kind=kLoop, calls=%fused_computation.100 | loop fusion | flops 14155776 | bytes 14155776 | tf_op jit(solution)/shard_map/reshape | solution.py:111
  184.2 233.4 %while.48 = (s32[]{:T(128)}, bf16[12,128,128]{2,1,0:T(8,128)(2,1)S(1)}, s32[12]{0:T(128)S(1)}, s32[2,27]{1,0:T(2,128)S(1)}, bf16[2,128,768]{2,1,0:T(8,128)(2,1)S...) while((s32[]{:T(128)}, ...), condition=%wide.region_4.5_spmd.clone, body=%wide.region_0.4_spmd.clone.sunk | while | flops 164492608 | bytes 10002113 | solution.py:186
  188.2 4.7 %select_reduce_fusion.2 = (pred[2304]{0:T(1024)(128)(4,1)S(1)}, pred[2304]{0:T(1024)(128)(4,1)S(1)}, pred[2304]{0:T(1024)(128)(4,1)S(1)}, pred[2304]{0:T(1024)(1...) fusion(pred[]{:T(512)} %bitcast.204, ...), kind=kLoop, calls=%fused_computation.55.clone.1 | loop fusion | flops 57600 | bytes 46087 | tf_op jit(solution)/shard_map/while/body/eval_jaxpr/jit(_take)/gather | solution.py:158
  192.9 7.0 %fusion.121 = pred[2304]{0:T(1024)(128)(4,1)S(1)} fusion(pred[2304]{0:T(1024)(128)(4,1)S(1)} %get-tuple-element.846, pred[2304]{0:T(1024)(128)(4,1)S(1)} %get-tuple-element.847, pred[2304]{0:T(1024)(128)(4,1)S(1)} %get-tuple-element.848, pred[2304]{0:T(1024)(128)(4,1)S(1)} %get-tuple-element.849, pred[2304]{0:T(1024)(128)(4,1)S(1)} %get-tuple-element.850, ...), kind=kLoop, calls=%fused_computation.79.clone.1 | loop fusion | flops 46080 | bytes 29963 | tf_op jit(solution)/shard_map/while/body/eval_jaxpr/jit(_take)/select_n | solution.py:158
  212.4 7.0 %fusion.121 = pred[2304]{0:T(1024)(128)(4,1)S(1)} fusion(pred[2304]{0:T(1024)(128)(4,1)S(1)} %get-tuple-element.846, pred[2304]{0:T(1024)(128)(4,1)S(1)} %get-tuple-element.847, pred[2304]{0:T(1024)(128)(4,1)S(1)} %get-tuple-element.848, pred[2304]{0:T(1024)(128)(4,1)S(1)} %get-tuple-element.849, pred[2304]{0:T(1024)(128)(4,1)S(1)} %get-tuple-element.850, ...), kind=kLoop, calls=%fused_computation.79.clone.1 | loop fusion | flops 46080 | bytes 29963 | tf_op jit(solution)/shard_map/while/body/eval_jaxpr/jit(_take)/select_n | solution.py:158
  227.1 4.7 %select_reduce_fusion.2 = (pred[2304]{0:T(1024)(128)(4,1)S(1)}, pred[2304]{0:T(1024)(128)(4,1)S(1)}, pred[2304]{0:T(1024)(128)(4,1)S(1)}, pred[2304]{0:T(1024)(1...) fusion(pred[]{:T(512)} %bitcast.204, ...), kind=kLoop, calls=%fused_computation.55.clone.1 | loop fusion | flops 57600 | bytes 46087 | tf_op jit(solution)/shard_map/while/body/eval_jaxpr/jit(_take)/gather | solution.py:158
  231.8 7.0 %fusion.121 = pred[2304]{0:T(1024)(128)(4,1)S(1)} fusion(pred[2304]{0:T(1024)(128)(4,1)S(1)} %get-tuple-element.846, pred[2304]{0:T(1024)(128)(4,1)S(1)} %get-tuple-element.847, pred[2304]{0:T(1024)(128)(4,1)S(1)} %get-tuple-element.848, pred[2304]{0:T(1024)(128)(4,1)S(1)} %get-tuple-element.849, pred[2304]{0:T(1024)(128)(4,1)S(1)} %get-tuple-element.850, ...), kind=kLoop, calls=%fused_computation.79.clone.1 | loop fusion | flops 46080 | bytes 29963 | tf_op jit(solution)/shard_map/while/body/eval_jaxpr/jit(_take)/select_n | solution.py:158
  246.6 4.7 %select_reduce_fusion.2 = (pred[2304]{0:T(1024)(128)(4,1)S(1)}, pred[2304]{0:T(1024)(128)(4,1)S(1)}, pred[2304]{0:T(1024)(128)(4,1)S(1)}, pred[2304]{0:T(1024)(1...) fusion(pred[]{:T(512)} %bitcast.204, ...), kind=kLoop, calls=%fused_computation.55.clone.1 | loop fusion | flops 57600 | bytes 46087 | tf_op jit(solution)/shard_map/while/body/eval_jaxpr/jit(_take)/gather | solution.py:158
  251.3 7.0 %fusion.121 = pred[2304]{0:T(1024)(128)(4,1)S(1)} fusion(pred[2304]{0:T(1024)(128)(4,1)S(1)} %get-tuple-element.846, pred[2304]{0:T(1024)(128)(4,1)S(1)} %get-tuple-element.847, pred[2304]{0:T(1024)(128)(4,1)S(1)} %get-tuple-element.848, pred[2304]{0:T(1024)(128)(4,1)S(1)} %get-tuple-element.849, pred[2304]{0:T(1024)(128)(4,1)S(1)} %get-tuple-element.850, ...), kind=kLoop, calls=%fused_computation.79.clone.1 | loop fusion | flops 46080 | bytes 29963 | tf_op jit(solution)/shard_map/while/body/eval_jaxpr/jit(_take)/select_n | solution.py:158
  270.7 7.0 %fusion.121 = pred[2304]{0:T(1024)(128)(4,1)S(1)} fusion(pred[2304]{0:T(1024)(128)(4,1)S(1)} %get-tuple-element.846, pred[2304]{0:T(1024)(128)(4,1)S(1)} %get-tuple-element.847, pred[2304]{0:T(1024)(128)(4,1)S(1)} %get-tuple-element.848, pred[2304]{0:T(1024)(128)(4,1)S(1)} %get-tuple-element.849, pred[2304]{0:T(1024)(128)(4,1)S(1)} %get-tuple-element.850, ...), kind=kLoop, calls=%fused_computation.79.clone.1 | loop fusion | flops 46080 | bytes 29963 | tf_op jit(solution)/shard_map/while/body/eval_jaxpr/jit(_take)/select_n | solution.py:158
  290.2 7.0 %fusion.121 = pred[2304]{0:T(1024)(128)(4,1)S(1)} fusion(pred[2304]{0:T(1024)(128)(4,1)S(1)} %get-tuple-element.846, pred[2304]{0:T(1024)(128)(4,1)S(1)} %get-tuple-element.847, pred[2304]{0:T(1024)(128)(4,1)S(1)} %get-tuple-element.848, pred[2304]{0:T(1024)(128)(4,1)S(1)} %get-tuple-element.849, pred[2304]{0:T(1024)(128)(4,1)S(1)} %get-tuple-element.850, ...), kind=kLoop, calls=%fused_computation.79.clone.1 | loop fusion | flops 46080 | bytes 29963 | tf_op jit(solution)/shard_map/while/body/eval_jaxpr/jit(_take)/select_n | solution.py:158
  309.6 7.0 %fusion.121 = pred[2304]{0:T(1024)(128)(4,1)S(1)} fusion(pred[2304]{0:T(1024)(128)(4,1)S(1)} %get-tuple-element.846, pred[2304]{0:T(1024)(128)(4,1)S(1)} %get-tuple-element.847, pred[2304]{0:T(1024)(128)(4,1)S(1)} %get-tuple-element.848, pred[2304]{0:T(1024)(128)(4,1)S(1)} %get-tuple-element.849, pred[2304]{0:T(1024)(128)(4,1)S(1)} %get-tuple-element.850, ...), kind=kLoop, calls=%fused_computation.79.clone.1 | loop fusion | flops 46080 | bytes 29963 | tf_op jit(solution)/shard_map/while/body/eval_jaxpr/jit(_take)/select_n | solution.py:158
  329.1 7.0 %fusion.121 = pred[2304]{0:T(1024)(128)(4,1)S(1)} fusion(pred[2304]{0:T(1024)(128)(4,1)S(1)} %get-tuple-element.846, pred[2304]{0:T(1024)(128)(4,1)S(1)} %get-tuple-element.847, pred[2304]{0:T(1024)(128)(4,1)S(1)} %get-tuple-element.848, pred[2304]{0:T(1024)(128)(4,1)S(1)} %get-tuple-element.849, pred[2304]{0:T(1024)(128)(4,1)S(1)} %get-tuple-element.850, ...), kind=kLoop, calls=%fused_computation.79.clone.1 | loop fusion | flops 46080 | bytes 29963 | tf_op jit(solution)/shard_map/while/body/eval_jaxpr/jit(_take)/select_n | solution.py:158
  348.5 7.0 %fusion.121 = pred[2304]{0:T(1024)(128)(4,1)S(1)} fusion(pred[2304]{0:T(1024)(128)(4,1)S(1)} %get-tuple-element.846, pred[2304]{0:T(1024)(128)(4,1)S(1)} %get-tuple-element.847, pred[2304]{0:T(1024)(128)(4,1)S(1)} %get-tuple-element.848, pred[2304]{0:T(1024)(128)(4,1)S(1)} %get-tuple-element.849, pred[2304]{0:T(1024)(128)(4,1)S(1)} %get-tuple-element.850, ...), kind=kLoop, calls=%fused_computation.79.clone.1 | loop fusion | flops 46080 | bytes 29963 | tf_op jit(solution)/shard_map/while/body/eval_jaxpr/jit(_take)/select_n | solution.py:158
  368.0 7.0 %fusion.121 = pred[2304]{0:T(1024)(128)(4,1)S(1)} fusion(pred[2304]{0:T(1024)(128)(4,1)S(1)} %get-tuple-element.846, pred[2304]{0:T(1024)(128)(4,1)S(1)} %get-tuple-element.847, pred[2304]{0:T(1024)(128)(4,1)S(1)} %get-tuple-element.848, pred[2304]{0:T(1024)(128)(4,1)S(1)} %get-tuple-element.849, pred[2304]{0:T(1024)(128)(4,1)S(1)} %get-tuple-element.850, ...), kind=kLoop, calls=%fused_computation.79.clone.1 | loop fusion | flops 46080 | bytes 29963 | tf_op jit(solution)/shard_map/while/body/eval_jaxpr/jit(_take)/select_n | solution.py:158
  387.4 7.0 %fusion.121 = pred[2304]{0:T(1024)(128)(4,1)S(1)} fusion(pred[2304]{0:T(1024)(128)(4,1)S(1)} %get-tuple-element.846, pred[2304]{0:T(1024)(128)(4,1)S(1)} %get-tuple-element.847, pred[2304]{0:T(1024)(128)(4,1)S(1)} %get-tuple-element.848, pred[2304]{0:T(1024)(128)(4,1)S(1)} %get-tuple-element.849, pred[2304]{0:T(1024)(128)(4,1)S(1)} %get-tuple-element.850, ...), kind=kLoop, calls=%fused_computation.79.clone.1 | loop fusion | flops 46080 | bytes 29963 | tf_op jit(solution)/shard_map/while/body/eval_jaxpr/jit(_take)/select_n | solution.py:158
  406.9 7.0 %fusion.121 = pred[2304]{0:T(1024)(128)(4,1)S(1)} fusion(pred[2304]{0:T(1024)(128)(4,1)S(1)} %get-tuple-element.846, pred[2304]{0:T(1024)(128)(4,1)S(1)} %get-tuple-element.847, pred[2304]{0:T(1024)(128)(4,1)S(1)} %get-tuple-element.848, pred[2304]{0:T(1024)(128)(4,1)S(1)} %get-tuple-element.849, pred[2304]{0:T(1024)(128)(4,1)S(1)} %get-tuple-element.850, ...), kind=kLoop, calls=%fused_computation.79.clone.1 | loop fusion | flops 46080 | bytes 29963 | tf_op jit(solution)/shard_map/while/body/eval_jaxpr/jit(_take)/select_n | solution.py:158
  (392 shorter events, 162.0 us)
Async XLA Ops:
  7.2 135.0 %all-reduce.4.cloned.1.call-start = ((), (), s32[]{:S(2)}) async-start(), calls=%async_computation | async-start | bytes 786432 | tf_op jit(solution)/shard_map/psum | solution.py:102
  8.4 60.2 %collective-permute-start = (bf16[1,1,2,2,8,16,768]{6,5,4,3,2,1,0:T(8,128)(2,1)S(1)}, bf16[1,1,2,2,8,16,768]{6,5,4,3,2,1,0:T(8,128)(2,1)S(1)}, u32[]{:S(2)}, u32[]{:S(2)}) collective-permute-start(bf16[1,1,2,2,8,16,768]{6,5,4,3,2,1,0:T(8,128)(2,1)S(1)} %maximum_bitcast_fusion.1), channel_id=1, source_target_pairs={{0,4},{4,8},{8,12},{1,5},{5,9},{9,13},{2,6},{6,10},{10,14},{3,7},{... | collective-permute-start | bytes 2359304 | tf_op jit(solution)/shard_map/ppermute | solution.py:16
  13.4 55.2 %collective-permute-start.1 = (bf16[1,1,2,2,8,16,768]{6,5,4,3,2,1,0:T(8,128)(2,1)S(1)}, bf16[1,1,2,2,8,16,768]{6,5,4,3,2,1,0:T(8,128)(2,1)S(1)}, u32[]{:S(2)}, u32[]{:S(2)}) collective-permute-start(bf16[1,1,2,2,8,16,768]{6,5,4,3,2,1,0:T(8,128)(2,1)S(1)} %maximum_bitcast_fusion.1), channel_id=1, source_target_pairs={{4,0},{8,4},{12,8},{5,1},{9,5},{13,9},{6,2},{10,6},{14,10},{7,3},{... | collective-permute-start | bytes 2359304 | tf_op jit(solution)/shard_map/ppermute | solution.py:17
  67.8 108.9 %all-reduce.6.cloned.1.call-start = ((), (), s32[]{:S(2)}) async-start(), calls=%async_computation.1 | async-start | bytes 786432 | tf_op jit(solution)/shard_map/psum | solution.py:103
  68.6 5.8 %copy-start.2 = (bf16[128,768]{1,0:T(8,128)(2,1)S(1)}, bf16[128,768]{1,0:T(8,128)(2,1)}, u32[]{:S(2)}) copy-start(bf16[128,768]{1,0:T(8,128)(2,1)} %param.20) | copy-start | bytes 589828
  68.6 73.5 %copy-start = (bf16[2,8,16,768]{3,2,1,0:T(8,128)(2,1)S(1)}, bf16[2,8,16,768]{3,2,1,0:T(8,128)(2,1)}, u32[]{:S(2)}) copy-start(bf16[2,8,16,768]{3,2,1,0:T(8,128)(2,1)} %param.15) | copy-start | bytes 1179652
  70.3 71.9 %copy-start.3 = (s32[1,1,2,26]{3,2,1,0:T(2,128)S(1)}, s32[1,1,2,26]{3,2,1,0:T(2,128)}, u32[]{:S(2)}) copy-start(s32[1,1,2,26]{3,2,1,0:T(2,128)} %param.21) | copy-start | bytes 628
  70.3 108.0 %collective-permute-start.2 = (bf16[3,1,2,2,8,16,768]{6,5,4,3,2,1,0:T(8,128)(2,1)}, bf16[3,1,2,2,8,16,768]{6,5,4,3,2,1,0:T(8,128)(2,1)}, u32[]{:S(2)}, u32[]{:S(2)}) collective-permute-start(bf16[3,1,2,2,8,16,768]{6,5,4,3,2,1,0:T(8,128)(2,1)} %pad_maximum_fusion), channel_id=1, source_target_pairs={{0,2},{1,3},{4,6},{5,7},{8,10},{9,11},{12,14},{13,15},{16,18},{17,... | collective-permute-start | bytes 7077896 | tf_op jit(solution)/shard_map/ppermute | solution.py:16
  73.1 105.2 %collective-permute-start.3 = (bf16[3,1,2,2,8,16,768]{6,5,4,3,2,1,0:T(8,128)(2,1)}, bf16[3,1,2,2,8,16,768]{6,5,4,3,2,1,0:T(8,128)(2,1)}, u32[]{:S(2)}, u32[]{:S(2)}) collective-permute-start(bf16[3,1,2,2,8,16,768]{6,5,4,3,2,1,0:T(8,128)(2,1)} %pad_maximum_fusion), channel_id=1, source_target_pairs={{2,0},{3,1},{6,4},{7,5},{10,8},{11,9},{14,12},{15,13},{18,16},{19,... | collective-permute-start | bytes 7077896 | tf_op jit(solution)/shard_map/ppermute | solution.py:17
  178.3 5.9 %copy-start.1 = (bf16[12,128,128]{2,1,0:T(8,128)(2,1)S(1)}, bf16[12,128,128]{2,1,0:T(8,128)(2,1)}, u32[]{:S(2)}) copy-start(bf16[12,128,128]{2,1,0:T(8,128)(2,1)} %custom-call.6) | copy-start | bytes 1179652
Sparse Core Ops, SparseCore 0:
  67.9 31.7 all-reduce.3
  142.3 34.2 all-reduce.5
